TPU v7x, 1024 devices: a whole 8x8x8 slice. The times are simulated.
1024 devices in a mesh: sec: 32 (over x, z_lo, core), row: 4 (over z_hi), col: 8 (over y).
Axes of the slice: x: 8, y: 8, z: 8 (z_hi: 4, z_lo: 2; z = z_hi * 2 + z_lo), core: 2. Of those that a mesh axis runs over, the one named last changes fastest.
Arguments:
- amplitudes: bfloat16 [32, 2, 512, 8192], P('sec', None, 'row', 'col'), may hold values from -0.25 to 0.25, as said below
- state_energies: float32 [32, 8192], P('sec', 'col'), may hold values from 1.25 to 12
- radii_table: int32 [33], replicated, may hold values from 20 to 532, as said below
- plan: int32 [32, 2], P('sec'), may hold values from 0 to 31, as said below
- entry_r: float32 [32, 512, 512], P('sec', 'col', 'row'), may hold values from -16 to 48, as said below
- fresh_r: float32 [1, 512, 512], P(None, 'col', 'row'), may hold values from -16 to 48, as said below
Outputs:
- exit_r: float32 [2, 32, 512, 512], P(None, 'sec', 'col', 'row')
Inputs may be any that keep to these rules, and one draw needn't show every extreme that they name: Each sector's outer-boundary amplitudes are correlated with its inner-boundary ones. `radii_table`: strictly increasing; consecutive radii differ by 4 to 16; the first is at least 20 and the last equals 532. plan[s, t] equals plan[s-1, t-1] for s, t >= 1. `entry_r`: symmetric positive definite, every eigenvalue at least 0.5. `fresh_r`: symmetric positive definite, every eigenvalue at least 0.5.
All inputs are finite; a program needn't handle non-finite values.
Results may differ from a plain program's by a relative error of at most 0.0016.
Values may be sent and summed in bfloat16 or wider, within the bound.
No kernel may reach another device: no remote copies, remote signals or barrier semaphores. Data moves between devices by JAX's collectives and lax.ppermute only.
A program may use at most 32 MiB of HBM per device.

v0:
```python
import jax
import jax.numpy as jnp
from jax import lax
from jax.sharding import PartitionSpec as P

ENERGIES = 32
TICKS = 2


def shifted_2(block, axis, distance):
    devices = range(lax.axis_size(axis))
    route = [(i - distance, i) for i in devices if i - distance in devices]
    return lax.ppermute(block, axis, route)


def contract(left_rows, right_rows, paired_panels, right_panel):
    contraction = (((1,), (1,)), ((), ()))
    paired_out = lax.dot_general(
        left_rows, paired_panels, contraction, preferred_element_type=jnp.float32
    )
    right_out = lax.dot_general(
        right_rows, right_panel, contraction, preferred_element_type=jnp.float32
    )
    return jnp.concatenate([paired_out, right_out], 1)


def assemble(stacked, row_count, col_count):
    tile_rows = stacked.shape[1]
    tile_cols = stacked.shape[2]
    grid = stacked.reshape(row_count, col_count, tile_rows, tile_cols)
    return grid.transpose(1, 2, 0, 3).reshape(col_count * tile_rows, row_count * tile_cols)


def local(amplitudes, state_energies, radii_table, plan, entry_r, fresh_r):
    sec_index = lax.axis_index("sec")
    row_index = lax.axis_index("row")
    col_index = lax.axis_index("col")
    row_count = lax.axis_size("row")
    col_count = lax.axis_size("col")
    local_panels = amplitudes[0]
    col_block = local_panels.shape[1]
    all_panels = lax.all_gather(local_panels, "row", axis=1, tiled=True)
    channels = all_panels.shape[1]
    row_block = channels // col_count
    paired_panels = local_panels.reshape(2 * col_block, local_panels.shape[2])
    bounds = lax.dynamic_slice_in_dim(radii_table, sec_index, 2)
    sector_width = (bounds[1] - bounds[0]).astype(jnp.float32)
    levels = state_energies[0]
    boundary = entry_r[0]
    results = []
    for period in range(TICKS):
        energy = plan[0, period].astype(jnp.float32) / ENERGIES
        weight = 8.0 / (sector_width * (levels - energy))
        scaled = (all_panels.astype(jnp.float32) * weight).astype(jnp.bfloat16)
        left_rows = scaled[0]
        right_rows = scaled[1]
        blocks = lax.psum_scatter(
            contract(left_rows, right_rows, paired_panels, local_panels[1]),
            "col",
            scatter_dimension=0,
            tiled=True,
        )
        system_tile = blocks[:, :col_block] + boundary
        cross_tile = blocks[:, col_block : 2 * col_block]
        gathered = (
            lax.all_gather(system_tile[None], ("row", "col"), axis=0, tiled=True),
            lax.all_gather(cross_tile[None], ("row", "col"), axis=0, tiled=True),
        )
        full_system = assemble(gathered[0], row_count, col_count)
        full_cross = assemble(gathered[1], row_count, col_count)
        green_tile = blocks[:, 2 * col_block :]
        factor = jnp.linalg.cholesky(full_system)
        needed = jnp.concatenate(
            [
                lax.dynamic_slice_in_dim(full_cross, col_index * row_block, row_block, 1),
                lax.dynamic_slice_in_dim(full_cross, row_index * col_block, col_block, 1),
            ],
            1,
        )
        solved = jax.scipy.linalg.solve_triangular(factor, needed, lower=True)
        exit_tile = green_tile - jnp.dot(
            solved[:, :row_block].T, solved[:, row_block:], precision=lax.Precision.HIGHEST
        )
        results.append(exit_tile)
        if period + 1 < TICKS:
            shifted = shifted_2(exit_tile, "sec", 1)
            boundary = jnp.where(sec_index == 0, fresh_r[period], shifted)
    return jnp.stack(results, 0)[:, None]


def solution(mesh):
    placed = (
        P("sec", None, "row", "col"),
        P("sec", "col"),
        P(),
        P("sec", None),
        P("sec", "col", "row"),
        P(None, "col", "row"),
    )
    return jax.shard_map(
        local, mesh=mesh, in_specs=placed, out_specs=P(None, "sec", "col", "row"), check_vma=False
    )
```

profile of v0, /device:TPU:6, one launch (start us, length us, event | category | flops | bytes accessed | tf_op | source)
XLA Modules:
  0.0 784.3 jit_solution(10816576137823754184)
XLA Ops:
  13.2 66.6 %all-gather.11.cloned.1.call-done = bf16[1,2,512,1024]{3,2,1,0:T(8,128)(2,1)} async-done(((bf16[1,2,128,1024]{3,2,1,0:T(8,128)(2,1)}), bf16[1,2,512,1024]{3,2,1,0:T(8,128)(2,1)}) %all-gather.11.cloned.1.call-update) | async-done | bytes 2097168 | tf_op jit(solution)/shard_map/all_gather | solution.py:42
  84.8 41.4 %reduce-scatter.7.cloned.1.call-done = f32[64,384]{1,0:T(8,128)} async-done(((f32[512,384]{1,0:T(8,128)}), f32[64,384]{1,0:T(8,128)}) %reduce-scatter.7.cloned.1.call-update) | async-done | bytes 98320 | tf_op jit(solution)/shard_map/reduce_scatter | solution.py:57
  131.3 90.4 %all-gather.15.cloned.1.call-done = f32[2048,128]{1,0:T(8,128)} async-done(((f32[64,128]{1,0:T(8,128)}), f32[2048,128]{1,0:T(8,128)}) %all-gather.15.cloned.1.call-update) | async-done | bytes 1048592 | tf_op jit(solution)/shard_map/all_gather | solution.py:67
  224.2 89.4 %all-gather.13.cloned.1.call-done = f32[2048,128]{1,0:T(8,128)} async-done(((f32[64,128]{1,0:T(8,128)}), f32[2048,128]{1,0:T(8,128)}) %all-gather.13.cloned.1.call-update) | async-done | bytes 1048592 | tf_op jit(solution)/shard_map/all_gather | solution.py:66
  316.2 11.7 %cholesky.286 = f32[128,128]{1,0:T(8,128)S(1)} custom-call(f32[128,128]{1,0:T(8,128)S(1)} %cholesky.426), custom_call_target="Cholesky" | custom-call | tf_op jit(solution)/shard_map/jit(cholesky)/cholesky | solution.py:72
  328.0 9.8 %custom-call.27 = f32[1,128,128]{1,2,0:T(8,128)S(1)} custom-call(f32[1,128,128]{2,1,0:T(8,128)S(1)} %get-tuple-element.68), custom_call_target="InvertDiagBlocksLowerTriangular" | custom-call | tf_op jit(solution)/shard_map/jit(cholesky)/cholesky | solution.py:72
  338.5 12.3 %cholesky.305 = f32[128,128]{1,0:T(8,128)S(1)} custom-call(f32[128,128]{1,0:T(8,128)S(1)} %cholesky.430), custom_call_target="Cholesky" | custom-call | tf_op jit(solution)/shard_map/jit(cholesky)/cholesky | solution.py:72
  350.8 9.8 %custom-call.28 = f32[1,128,128]{1,2,0:T(8,128)S(1)} custom-call(f32[1,128,128]{2,1,0:T(8,128)S(1)} %get-tuple-element.65), custom_call_target="InvertDiagBlocksLowerTriangular" | custom-call | tf_op jit(solution)/shard_map/jit(cholesky)/cholesky | solution.py:72
  361.3 11.7 %cholesky.326 = f32[128,128]{1,0:T(8,128)S(1)} custom-call(f32[128,128]{1,0:T(8,128)S(1)} %cholesky.435), custom_call_target="Cholesky" | custom-call | tf_op jit(solution)/shard_map/jit(cholesky)/cholesky | solution.py:72
  373.1 9.8 %custom-call.29 = f32[1,128,128]{1,2,0:T(8,128)S(1)} custom-call(f32[1,128,128]{2,1,0:T(8,128)S(1)} %get-tuple-element.62), custom_call_target="InvertDiagBlocksLowerTriangular" | custom-call | tf_op jit(solution)/shard_map/jit(cholesky)/cholesky | solution.py:72
  383.5 11.8 %cholesky.343 = f32[128,128]{1,0:T(8,128)S(1)} custom-call(f32[128,128]{1,0:T(8,128)S(1)} %convolution_subtract_fusion.11), custom_call_target="Cholesky" | custom-call | tf_op jit(solution)/shard_map/jit(cholesky)/cholesky | solution.py:72
  400.2 7.7 while.4
  407.9 39.3 %custom-call.30 = f32[4,128,128]{1,2,0:T(8,128)S(1)} custom-call(f32[4,128,128]{2,1,0:T(8,128)S(1)} %get-tuple-element.21), custom_call_target="InvertDiagBlocksLowerTriangular" | custom-call | tf_op jit(solution)/shard_map/jit(_solve_triangular)/triangular_solve | solution.py:80
  458.8 88.3 %all-gather.19.cloned.1.call-done = f32[2048,128]{1,0:T(8,128)} async-done(((f32[64,128]{1,0:T(8,128)}), f32[2048,128]{1,0:T(8,128)}) %all-gather.19.cloned.1.call-update) | async-done | bytes 1048592 | tf_op jit(solution)/shard_map/all_gather | solution.py:67
  549.6 89.6 %all-gather.17.cloned.1.call-done = f32[2048,128]{1,0:T(8,128)} async-done(((f32[64,128]{1,0:T(8,128)}), f32[2048,128]{1,0:T(8,128)}) %all-gather.17.cloned.1.call-update) | async-done | bytes 1048592 | tf_op jit(solution)/shard_map/all_gather | solution.py:66
  641.7 11.7 %cholesky.358 = f32[128,128]{1,0:T(8,128)S(1)} custom-call(f32[128,128]{1,0:T(8,128)S(1)} %cholesky.439), custom_call_target="Cholesky" | custom-call | tf_op jit(solution)/shard_map/jit(cholesky)/cholesky | solution.py:72
  653.6 9.8 %custom-call.31 = f32[1,128,128]{1,2,0:T(8,128)S(1)} custom-call(f32[1,128,128]{2,1,0:T(8,128)S(1)} %get-tuple-element.58), custom_call_target="InvertDiagBlocksLowerTriangular" | custom-call | tf_op jit(solution)/shard_map/jit(cholesky)/cholesky | solution.py:72
  664.1 12.1 %cholesky.377 = f32[128,128]{1,0:T(8,128)S(1)} custom-call(f32[128,128]{1,0:T(8,128)S(1)} %cholesky.443), custom_call_target="Cholesky" | custom-call | tf_op jit(solution)/shard_map/jit(cholesky)/cholesky | solution.py:72
  676.2 9.8 %custom-call.32 = f32[1,128,128]{1,2,0:T(8,128)S(1)} custom-call(f32[1,128,128]{2,1,0:T(8,128)S(1)} %get-tuple-element.55), custom_call_target="InvertDiagBlocksLowerTriangular" | custom-call | tf_op jit(solution)/shard_map/jit(cholesky)/cholesky | solution.py:72
  686.7 11.7 %cholesky.398 = f32[128,128]{1,0:T(8,128)S(1)} custom-call(f32[128,128]{1,0:T(8,128)S(1)} %cholesky.448), custom_call_target="Cholesky" | custom-call | tf_op jit(solution)/shard_map/jit(cholesky)/cholesky | solution.py:72
  698.5 9.8 %custom-call.33 = f32[1,128,128]{1,2,0:T(8,128)S(1)} custom-call(f32[1,128,128]{2,1,0:T(8,128)S(1)} %get-tuple-element.52), custom_call_target="InvertDiagBlocksLowerTriangular" | custom-call | tf_op jit(solution)/shard_map/jit(cholesky)/cholesky | solution.py:72
  708.9 11.9 %cholesky.415 = f32[128,128]{1,0:T(8,128)S(1)} custom-call(f32[128,128]{1,0:T(8,128)S(1)} %convolution_subtract_fusion.10), custom_call_target="Cholesky" | custom-call | tf_op jit(solution)/shard_map/jit(cholesky)/cholesky | solution.py:72
  726.0 8.1 %while.5 = (s32[]{:T(128)}, f32[512,512]{1,0:T(8,128)S(1)}, s32[4,2]{0,1:T(2,128)S(1)}, f32[4,128,128]{2,1,0:T(8,128)S(1)}, s32[]{:T(128)}) while((s32[]{:T(128)}, f32[512,512]{1,0:T(8,128)S(1)}, s32[4,2]{0,1:T(2,128)S(1)}, f32[4,128,128]{2,1,0:T(8,128)S(1)}, s32[]{:T(128)}) %tuple.77), condition=%wide.while_cond.clone, body=%wide.while_body.clone.sunk | while | flops 2 | bytes 131189 | solution.py:80
  734.1 39.3 %custom-call.34 = f32[4,128,128]{1,2,0:T(8,128)S(1)} custom-call(f32[4,128,128]{2,1,0:T(8,128)S(1)} %get-tuple-element.22), custom_call_target="InvertDiagBlocksLowerTriangular" | custom-call | tf_op jit(solution)/shard_map/jit(_solve_triangular)/triangular_solve | solution.py:80
  (144 shorter events, 64.0 us)
Async XLA Ops:
  6.5 73.3 %all-gather.11.cloned.1.call-start = ((), (), s32[]{:S(2)}) async-start(), calls=%async_computation.2 | async-start | bytes 2621440 | tf_op jit(solution)/shard_map/all_gather | solution.py:42
  7.3 119.0 %reduce-scatter.7.cloned.1.call-start = ((), (), s32[]{:S(2)}) async-start(), calls=%async_computation.7 | async-start | bytes 884736 | tf_op jit(solution)/shard_map/reduce_scatter | solution.py:57
  79.8 2.7 copy-start
  83.5 44.2 %copy-start.3 = (f32[1,64,128]{2,1,0:T(8,128)S(1)}, f32[1,64,128]{2,1,0:T(8,128)}, u32[]{:S(2)}) copy-start(f32[1,64,128]{2,1,0:T(8,128)} %param.13) | copy-start | bytes 98308
  84.8 136.9 %all-gather.15.cloned.1.call-start = ((), (), s32[]{:S(2)}) async-start(), calls=%async_computation.4 | async-start | bytes 1081344 | tf_op jit(solution)/shard_map/all_gather | solution.py:67
  127.6 186.0 %all-gather.13.cloned.1.call-start = ((), (), s32[]{:S(2)}) async-start(), calls=%async_computation.3 | async-start | bytes 1081344 | tf_op jit(solution)/shard_map/all_gather | solution.py:66
  128.6 323.8 %reduce-scatter.9.cloned.1.call-start = ((), (), s32[]{:S(2)}) async-start(), calls=%async_computation.8 | async-start | bytes 884736 | tf_op jit(solution)/shard_map/reduce_scatter | solution.py:57
  130.9 416.2 %all-gather.19.cloned.1.call-start = ((), (), s32[]{:S(2)}) async-start(), calls=%async_computation.6 | async-start | bytes 1081344 | tf_op jit(solution)/shard_map/all_gather | solution.py:67
  447.5 9.1 %copy-start.4 = (f32[1,64,128]{2,1,0:T(8,128)S(1)}, f32[1,64,128]{2,1,0:T(8,128)}, u32[]{:S(2)}) copy-start(f32[1,64,128]{2,1,0:T(8,128)} %param.14) | copy-start | bytes 98308
  450.4 96.6 %copy-start.1 = (f32[64,128]{1,0:T(8,128)}, f32[64,128]{1,0:T(8,128)S(1)}, u32[]{:S(2)}) copy-start(f32[64,128]{1,0:T(8,128)S(1)} %convolution_subtract_fusion.13) | copy-start | bytes 98308
  450.4 6.1 collective-permute-start
  458.0 181.1 %all-gather.17.cloned.1.call-start = ((), (), s32[]{:S(2)}) async-start(), calls=%async_computation.5 | async-start | bytes 1081344 | tf_op jit(solution)/shard_map/all_gather | solution.py:66
  773.7 2.9 copy-start.2
Sparse Core Ops, SparseCore 0:
  10.0 69.7 all-gather.10
  84.9 41.2 reduce-scatter.6
  130.6 91.0 all-gather.14
  225.9 87.6 all-gather.12
  316.8 39.8 reduce-scatter.8
  458.1 88.9 all-gather.18
  551.4 87.6 all-gather.16
where the time goes:
time: 788 us; the launch traced here: 784 us
  waiting for transfers between devices  471 us (60%)
  other arithmetic  244 us (31%)
  local copies, waits for them, and re-layouts  32.8 us (4%)
  between operations  21.9 us (3%)
  matrix products  11.9 us (2%)
    all_gather x2, waiting for transfers between devices, local(): lax.all_gather(system_tile[None], ('row', 'col'), axis=0, tiled=True)  179 us
    all_gather x2, waiting for transfers between devices, local(): lax.all_gather(cross_tile[None], ('row', 'col'), axis=0, tiled=True)  179 us
    another operation x29, other arithmetic, local(): factor = jnp.linalg.cholesky(full_system)  159 us
    another operation x5, other arithmetic, local(): solved = jax.scipy.linalg.solve_triangular(factor, needed, lower=True)  78.9 us
    all_gather x1, waiting for transfers between devices, local(): all_panels = lax.all_gather(local_panels, 'row', axis=1, tiled=True)  66.6 us
    reduce_scatter x2, waiting for transfers between devices, local(): lax.psum_scatter(contract(left_rows, right_rows, paired_panels, local_pan...  41.4 us
  transfers between devices with their start and end apart: 8, of which 7 were waited for; matrix products, arithmetic and copies ran while one was open for 19% of the time, Pallas kernels for 0%

commit v1 on v0

v1 whole, which is shorter than its diff:
```python
import jax
import jax.numpy as jnp
from jax import lax
from jax.experimental import pallas as pl
from jax.experimental.pallas import tpu as pltpu
from jax.sharding import PartitionSpec as P

ENERGIES = 32
TICKS = 2
BLOCK = 128
GROUP = 8


def dot_nt(left, right):
    return lax.dot_general(
        left,
        right,
        (((1,), (1,)), ((), ())),
        precision=lax.Precision.HIGHEST,
        preferred_element_type=jnp.float32,
    )


def across_lanes(tile, lane):
    return jnp.broadcast_to(tile[:, lane : lane + 1], (8, BLOCK))


def across_sublanes(tile, row):
    return jnp.broadcast_to(tile[row : row + 1, :], (8, BLOCK))


def inverse_factor(block):
    tiles = BLOCK // 8
    sub_id = lax.broadcasted_iota(jnp.int32, (8, BLOCK), 0)
    lane_id = lax.broadcasted_iota(jnp.int32, (8, BLOCK), 1)
    a = [block[8 * t : 8 * t + 8, :] for t in range(tiles)]
    e = [(lane_id == sub_id + 8 * t).astype(jnp.float32) for t in range(tiles)]
    out = [jnp.zeros((8, BLOCK), jnp.float32) for _ in range(tiles)]
    for first in range(0, BLOCK, GROUP):
        top, off = first // 8, first % 8
        col = {
            (t, j): across_lanes(a[t], first + j) for t in range(top, tiles) for j in range(GROUP)
        }
        s = {(i, j): across_sublanes(col[top, j], off + i) for i in range(GROUP) for j in range(i + 1)}
        row_a = [across_sublanes(a[top], off + i) for i in range(GROUP)]
        row_e = [across_sublanes(e[top], off + i) for i in range(GROUP)]
        inv = [None] * GROUP
        low = {}
        for i in range(GROUP):
            inv[i] = 1.0 / s[i, i]
            for j in range(i + 1, GROUP):
                low[j, i] = s[j, i] * inv[i]
            for j in range(i + 1, GROUP):
                for q in range(i + 1, j + 1):
                    s[j, q] = s[j, q] - low[j, i] * s[q, i]
                row_a[j] = row_a[j] - low[j, i] * row_a[i]
                row_e[j] = row_e[j] - low[j, i] * row_e[i]
            out[top] = jnp.where(sub_id == off + i, row_e[i] * lax.rsqrt(s[i, i]), out[top])
        up_a = [None] * GROUP
        up_e = [None] * GROUP
        for i in reversed(range(GROUP)):
            up_a[i] = row_a[i] * inv[i]
            up_e[i] = row_e[i] * inv[i]
            for j in range(i + 1, GROUP):
                up_a[i] = up_a[i] - low[j, i] * up_a[j]
                up_e[i] = up_e[i] - low[j, i] * up_e[j]
        for t in range((first + GROUP) // 8, tiles):
            for j in range(GROUP):
                c = col[t, j]
                if t == top:
                    c = jnp.where(sub_id >= off + GROUP, c, 0.0)
                a[t] = a[t] - c * up_a[j]
                e[t] = e[t] - c * up_e[j]
    return jnp.concatenate(out, 0)


def exit_kernel(system_ref, right_ref, left_ref, green_ref, out_ref, work):
    count = work.shape[0]
    rows = system_ref.shape[1]
    col_count = system_ref.shape[0] // count
    per = BLOCK // rows

    def raw(i, j):
        return jnp.concatenate(
            [system_ref[j * col_count + per * i + p] for p in range(per)], 0
        )

    size = count * BLOCK
    for j in range(count):
        for i in range(j, count):
            work[j, i * BLOCK : (i + 1) * BLOCK, :] = 0.5 * (raw(i, j) + raw(j, i).T)
        chunk = jnp.concatenate([right_ref[per * j + p] for p in range(per)], 0)
        work[j, size : size + BLOCK, :] = chunk.T
        work[j, size + BLOCK : size + BLOCK + rows, :] = left_ref[j]
    for k in range(count):
        begin = k * BLOCK
        inverse = inverse_factor(work[k, begin : begin + BLOCK, :])
        panel = dot_nt(work[k, begin + BLOCK :, :], inverse)
        for j in range(k + 1, count):
            lead = (j - k - 1) * BLOCK
            work[j, j * BLOCK :, :] -= dot_nt(panel[lead:], panel[lead : lead + BLOCK])
        work[k, size:, :] = panel[size - begin - BLOCK :]
    total = green_ref[...]
    for k in range(count):
        total -= dot_nt(work[k, size + BLOCK :, :], work[k, size : size + BLOCK, :])
    out_ref[...] = total


def exit_tile_of(system, right, left, green):
    rows = green.shape[0]
    count = left.shape[0]
    return pl.pallas_call(
        exit_kernel,
        out_shape=jax.ShapeDtypeStruct(green.shape, jnp.float32),
        scratch_shapes=[pltpu.VMEM((count, count * BLOCK + BLOCK + rows, BLOCK), jnp.float32)],
        cost_estimate=pl.CostEstimate(
            flops=600_000_000, bytes_accessed=2_000_000, transcendentals=0
        ),
        name="exit_tile",
    )(system, right, left, green)


def contract(left_rows, right_rows):
    return lax.dot_general(
        left_rows, right_rows, (((1,), (1,)), ((), ())), preferred_element_type=jnp.float32
    )


def spread(tile, axes, count):
    copies = jnp.broadcast_to(tile[None], (count,) + tile.shape)
    return lax.all_to_all(copies, axes, 0, 0)


def shifted(block, axis, distance):
    devices = range(lax.axis_size(axis))
    route = [(i - distance, i) for i in devices if i - distance in devices]
    return lax.ppermute(block, axis, route)


def local(amplitudes, state_energies, radii_table, plan, entry_r, fresh_r):
    sec_index = lax.axis_index("sec")
    row_count = lax.axis_size("row")
    col_count = lax.axis_size("col")
    own = amplitudes[0]
    tile = own.shape[1]
    gathered = spread(own, "row", row_count)
    everyone = gathered.transpose(1, 0, 2, 3).reshape(2, row_count * tile, own.shape[2])
    bounds = lax.dynamic_slice_in_dim(radii_table, sec_index, 2)
    sector_width = (bounds[1] - bounds[0]).astype(jnp.float32)
    levels = state_energies[0]

    def greens(period):
        energy = plan[0, period].astype(jnp.float32) / ENERGIES
        weight = 8.0 / (sector_width * (levels - energy))
        scaled = (everyone.astype(jnp.float32) * weight).astype(jnp.bfloat16)
        scaled_own = (own[0].astype(jnp.float32) * weight).astype(jnp.bfloat16)
        paired = own.reshape(2 * tile, own.shape[2])
        return jnp.concatenate(
            [
                contract(scaled[0], paired),
                contract(scaled[1], own[1]),
                contract(everyone[1], scaled_own),
            ],
            1,
        )

    results = []
    boundary = entry_r[0]
    later = [
        lax.psum_scatter(greens(period), "col", scatter_dimension=0, tiled=True)
        for period in range(1, TICKS)
    ]
    partial = greens(0)
    parts = lax.all_to_all(
        partial.reshape(col_count, -1, partial.shape[1]), "col", 0, 0
    )
    blocks = parts.sum(0)
    for period in range(TICKS):
        right = spread(blocks[:, tile : 2 * tile], "col", col_count)
        left = spread(blocks[:, 3 * tile :], "row", row_count)
        system = spread(
            blocks[:, :tile] + boundary, ("row", "col"), row_count * col_count
        )
        exit_tile = exit_tile_of(system, right, left, blocks[:, 2 * tile : 3 * tile])
        results.append(exit_tile)
        if period + 1 < TICKS:
            entering = shifted(exit_tile, "sec", 1)
            boundary = jnp.where(sec_index == 0, fresh_r[period], entering)
            blocks = later[period]
    return jnp.stack(results, 0)[:, None]


def solution(mesh):
    placed = (
        P("sec", None, "row", "col"),
        P("sec", "col"),
        P(),
        P("sec", None),
        P("sec", "col", "row"),
        P(None, "col", "row"),
    )
    return jax.shard_map(
        local, mesh=mesh, in_specs=placed, out_specs=P(None, "sec", "col", "row"), check_vma=False
    )
```

time: 788 us -> 322 us (0.41)
  the two profiles are of different devices: /device:TPU:6 before, /device:TPU:22 now
where the time goes in v1:
time: 322 us; the launch traced here: 317 us
  blocking collectives  96.3 us (30%)
  waiting for transfers between devices  71.8 us (22%)
  Pallas kernels  62 us (19%)
  starting transfers between devices  47.8 us (15%)
  between operations  16.4 us (5%)
  local copies, waits for them, and re-layouts  9.11 us (3%)
  other arithmetic  7.19 us (2%)
  matrix products  6.19 us (2%)
    all_to_all x4, waiting for transfers between devices, spread(): return lax.all_to_all(copies, axes, 0, 0)  67.4 us
    all_to_all x3, blocking collectives, spread(): return lax.all_to_all(copies, axes, 0, 0)  63.3 us
    pallas_call x2, Pallas kernels, exit_tile_of(): pl.pallas_call(exit_kernel, out_shape=jax.ShapeDtypeStruct(green.shape, j...  62 us
    all_to_all x4, starting transfers between devices, spread(): return lax.all_to_all(copies, axes, 0, 0)  45.5 us
    all_to_all x1, blocking collectives, local(): lax.all_to_all(partial.reshape(col_count, -1, partial.shape[1]), 'col', 0...  33 us
  transfers between devices with their start and end apart: 6, of which 5 were waited for; matrix products, arithmetic and copies ran while one was open for 2% of the time, Pallas kernels for 10%

profile of v1, /device:TPU:22, one launch (start us, length us, event | category | flops | bytes accessed | tf_op | source)
XLA Modules:
  0.0 316.8 jit_solution(16215822542013371526)
XLA Ops:
  6.5 2.6 broadcast_in_dim.19
  9.2 15.9 %all-to-all-start = ((bf16[4,2,128,1024]{3,2,1,0:T(8,128)(2,1)}), bf16[4,2,128,1024]{3,2,1,0:T(8,128)(2,1)S(1)}, u32[]{:S(2)}, u32[]{:S(2)}) async-start(bf16[4,2,128,1024]{3,2,1,0:T(8,128)(2,1)} %broadcast_in_dim.19), calls=%async_computation | async-start | bytes 4194304 | tf_op jit(solution)/shard_map/all_to_all | solution.py:131
  29.0 30.3 %all-to-all-done = bf16[4,2,128,1024]{3,2,1,0:T(8,128)(2,1)S(1)} async-done(((bf16[4,2,128,1024]{3,2,1,0:T(8,128)(2,1)}), bf16[4,2,128,1024]{3,2,1,0:T(8,128)(2,1)S(1)}, u32[]{:S(2)}, u32[]{:S(2)}) %all-to-all-start) | async-done | bytes 2097184 | tf_op jit(solution)/shard_map/all_to_all | solution.py:131
  61.0 2.5 fusion
  64.9 33.0 %all_to_all.40 = f32[8,64,512]{2,1,0:T(8,128)S(1)} all-to-all(f32[8,64,512]{2,1,0:T(8,128)S(1)} %bitcast.62), channel_id=1, replica_groups=mesh['sec'=32,'row'=4,'col'=8] {'col'}, dimensions={0} | all-to-all | bytes 2097152 | tf_op jit(solution)/shard_map/all_to_all | solution.py:174
  99.3 19.8 %all-to-all-start.4 = ((f32[4,64,128]{2,1,0:T(8,128)}), f32[4,64,128]{2,1,0:T(8,128)}, u32[]{:S(2)}, u32[]{:S(2)}) async-start(f32[4,64,128]{2,1,0:T(8,128)} %broadcast_in_dim.22), calls=%async_computation.4 | async-start | bytes 262144 | tf_op jit(solution)/shard_map/all_to_all | solution.py:131
  119.0 1.4 convolution_bitcast_fusion
  120.4 7.4 %all-to-all-done.4.left_ref = f32[4,64,128]{2,1,0:T(8,128)} async-done(((f32[4,64,128]{2,1,0:T(8,128)}), f32[4,64,128]{2,1,0:T(8,128)}, u32[]{:S(2)}, u32[]{:S(2)}) %all-to-all-start.4) | async-done | bytes 131104 | tf_op jit(solution)/shard_map/all_to_all | solution.py:131
  128.6 4.4 %all-to-all-start.3 = ((f32[8,64,128]{2,1,0:T(8,128)}), f32[8,64,128]{2,1,0:T(8,128)S(1)}, u32[]{:S(2)}, u32[]{:S(2)}) async-start(f32[8,64,128]{2,1,0:T(8,128)} %broadcast_in_dim.21), calls=%async_computation.3 | async-start | bytes 524288 | tf_op jit(solution)/shard_map/all_to_all | solution.py:131
  133.0 2.1 fusion.2
  135.1 1.3 fusion.3
  136.4 5.2 %all-to-all-done.3.right_ref = f32[8,64,128]{2,1,0:T(8,128)S(1)} async-done(((f32[8,64,128]{2,1,0:T(8,128)}), f32[8,64,128]{2,1,0:T(8,128)S(1)}, u32[]{:S(2)}, u32[]{:S(2)}) %all-to-all-start.3) | async-done | bytes 262176 | tf_op jit(solution)/shard_map/all_to_all | solution.py:131
  142.7 5.5 %all-to-all-start.2 = ((f32[32,64,128]{2,1,0:T(8,128)}), f32[32,64,128]{2,1,0:T(8,128)S(1)}, u32[]{:S(2)}, u32[]{:S(2)}) async-start(f32[32,64,128]{2,1,0:T(8,128)} %broadcast_in_dim.20), calls=%async_computation.2 | async-start | bytes 2097152 | tf_op jit(solution)/shard_map/all_to_all | solution.py:131
  148.6 1.1 pad_maximum_fusion.1
  149.7 24.4 %all-to-all-done.2.system_ref = f32[32,64,128]{2,1,0:T(8,128)S(1)} async-done(((f32[32,64,128]{2,1,0:T(8,128)}), f32[32,64,128]{2,1,0:T(8,128)S(1)}, u32[]{:S(2)}, u32[]{:S(2)}) %all-to-all-start.2) | async-done | bytes 1048608 | tf_op jit(solution)/shard_map/all_to_all | solution.py:131
  175.1 31.2 %exit_tile.2 = f32[64,128]{1,0:T(8,128)} custom-call(f32[32,64,128]{2,1,0:T(8,128)} %copy-done.3, f32[8,64,128]{2,1,0:T(8,128)} %copy-done.5, f32[4,64,128]{2,1,0:T(8,128)} %all-to-all-done.4.left_ref, f32[64,128]{1,0:T(8,128)} %get-tuple-element.13.green_ref), custom_call_target="tpu_custom_call" | custom-call | flops 600000000 | bytes 2000000 | tf_op jit(solution)/shard_map/exit_tile/pallas_call | solution.py:112
  206.2 1.9 collective-permute-start
  208.2 4.4 %collective-permute-done = f32[64,128]{1,0:T(8,128)S(1)} collective-permute-done((f32[64,128]{1,0:T(8,128)}, f32[64,128]{1,0:T(8,128)S(1)}, u32[]{:S(2)}, u32[]{:S(2)}) %collective-permute-start) | collective-permute-done | bytes 32800 | tf_op jit(solution)/shard_map/ppermute | solution.py:137
  212.5 1.4 fusion.21
  214.0 12.1 %all_to_all.41.left_ref = f32[4,64,128]{2,1,0:T(8,128)} all-to-all(f32[4,64,128]{2,1,0:T(8,128)S(1)} %broadcast_in_dim.25), channel_id=1, replica_groups=mesh['sec'=32,'row'=4,'col'=8] {'row'}, dimensions={0} | all-to-all | bytes 262144 | tf_op jit(solution)/shard_map/all_to_all | solution.py:131
  226.1 15.2 %all_to_all.42.right_ref = f32[8,64,128]{2,1,0:T(8,128)} all-to-all(f32[8,64,128]{2,1,0:T(8,128)S(1)} %broadcast_in_dim.24), channel_id=1, replica_groups=mesh['sec'=32,'row'=4,'col'=8] {'col'}, dimensions={0} | all-to-all | bytes 524288 | tf_op jit(solution)/shard_map/all_to_all | solution.py:131
  241.5 36.0 %all_to_all.43.system_ref = f32[32,64,128]{2,1,0:T(8,128)} all-to-all(f32[32,64,128]{2,1,0:T(8,128)S(1)} %broadcast_in_dim.23), channel_id=1, replica_groups=mesh['sec'=32,'row'=4,'col'=8] {'row','col'}, dimensions={0} | all-to-all | bytes 2097152 | tf_op jit(solution)/shard_map/all_to_all | solution.py:131
  277.4 30.8 %exit_tile.3 = f32[64,128]{1,0:T(8,128)} custom-call(f32[32,64,128]{2,1,0:T(8,128)} %all_to_all.43.system_ref, f32[8,64,128]{2,1,0:T(8,128)} %all_to_all.42.right_ref, f32[4,64,128]{2,1,0:T(8,128)} %all_to_all.41.left_ref, f32[64,128]{1,0:T(8,128)} %get-tuple-element.9.green_ref), custom_call_target="tpu_custom_call" | custom-call | flops 600000000 | bytes 2000000 | tf_op jit(solution)/shard_map/exit_tile/pallas_call | solution.py:112
  308.3 1.4 maximum_bitcast_fusion
  (48 shorter events, 9.1 us)
Async XLA Ops:
  9.2 15.9 %copy-start.12 = (s32[33]{0:T(128)S(1)}, s32[33]{0:T(128)}, u32[]{:S(2)}) copy-start(s32[33]{0:T(128)} %param.8) | copy-start | bytes 400
  9.2 17.9 %copy-start.11 = (s32[1,2]{1,0:T(1,128)S(1)}, s32[1,2]{1,0:T(1,128)}, u32[]{:S(2)}) copy-start(s32[1,2]{1,0:T(1,128)} %param.9) | copy-start | bytes 28
  9.2 19.8 %copy-start.10 = (f32[1,1024]{1,0:T(1,128)S(1)}, f32[1,1024]{1,0:T(1,128)}, u32[]{:S(2)}) copy-start(f32[1,1024]{1,0:T(1,128)} %param.7) | copy-start | bytes 12292
  9.2 50.1 %all-to-all-start = ((bf16[4,2,128,1024]{3,2,1,0:T(8,128)(2,1)}), bf16[4,2,128,1024]{3,2,1,0:T(8,128)(2,1)S(1)}, u32[]{:S(2)}, u32[]{:S(2)}) async-start(bf16[4,2,128,1024]{3,2,1,0:T(8,128)(2,1)} %broadcast_in_dim.19), calls=%async_computation | async-start | bytes 4194304 | tf_op jit(solution)/shard_map/all_to_all | solution.py:131
  59.5 1.0 copy-start.1
  64.9 33.0 %copy-start.7 = (f32[1,64,128]{2,1,0:T(8,128)S(1)}, f32[1,64,128]{2,1,0:T(8,128)}, u32[]{:S(2)}) copy-start(f32[1,64,128]{2,1,0:T(8,128)} %param.10) | copy-start | bytes 98308
  98.0 35.1 %copy-start = (bf16[2,512,1024]{2,1,0:T(8,128)(2,1)S(1)}, bf16[2,512,1024]{2,1,0:T(8,128)(2,1)}, u32[]{:S(2)}) copy-start(bf16[2,512,1024]{2,1,0:T(8,128)(2,1)} %get-tuple-element.6) | copy-start | bytes 6291460
  99.3 28.6 %all-to-all-start.4 = ((f32[4,64,128]{2,1,0:T(8,128)}), f32[4,64,128]{2,1,0:T(8,128)}, u32[]{:S(2)}, u32[]{:S(2)}) async-start(f32[4,64,128]{2,1,0:T(8,128)} %broadcast_in_dim.22), calls=%async_computation.4 | async-start | bytes 262144 | tf_op jit(solution)/shard_map/all_to_all | solution.py:131
  120.4 14.7 %copy-start.2 = (bf16[1,2,128,1024]{3,2,1,0:T(8,128)(2,1)S(1)}, bf16[1,2,128,1024]{3,2,1,0:T(8,128)(2,1)}, u32[]{:S(2)}) copy-start(bf16[1,2,128,1024]{3,2,1,0:T(8,128)(2,1)} %param.6) | copy-start | bytes 1572868
  128.6 13.1 %all-to-all-start.3 = ((f32[8,64,128]{2,1,0:T(8,128)}), f32[8,64,128]{2,1,0:T(8,128)S(1)}, u32[]{:S(2)}, u32[]{:S(2)}) async-start(f32[8,64,128]{2,1,0:T(8,128)} %broadcast_in_dim.21), calls=%async_computation.3 | async-start | bytes 524288 | tf_op jit(solution)/shard_map/all_to_all | solution.py:131
  136.4 12.1 %copy-start.4 = (f32[512,256]{1,0:T(8,128)S(1)}, f32[512,256]{1,0:T(8,128)}, u32[]{:S(2)}) copy-start(f32[512,256]{1,0:T(8,128)} %fusion.3) | copy-start | bytes 1572868
  136.4 12.1 %copy-start.6 = (f32[512,128]{1,0:T(8,128)S(1)}, f32[512,128]{1,0:T(8,128)}, u32[]{:S(2)}) copy-start(f32[512,128]{1,0:T(8,128)} %fusion.2) | copy-start | bytes 786436
  141.6 1.1 copy-start.5
  142.7 31.4 %all-to-all-start.2 = ((f32[32,64,128]{2,1,0:T(8,128)}), f32[32,64,128]{2,1,0:T(8,128)S(1)}, u32[]{:S(2)}, u32[]{:S(2)}) async-start(f32[32,64,128]{2,1,0:T(8,128)} %broadcast_in_dim.20), calls=%async_computation.2 | async-start | bytes 2097152 | tf_op jit(solution)/shard_map/all_to_all | solution.py:131
  148.2 60.0 %reduce-scatter.2.cloned.1.call-start = ((), (), s32[]{:S(2)}) async-start(), calls=%async_computation.9 | async-start | bytes 1179648 | tf_op jit(solution)/shard_map/reduce_scatter | solution.py:170
  149.6 62.9 %copy-start.8 = (f32[1,64,128]{2,1,0:T(8,128)S(1)}, f32[1,64,128]{2,1,0:T(8,128)}, u32[]{:S(2)}) copy-start(f32[1,64,128]{2,1,0:T(8,128)} %param.11) | copy-start | bytes 98308
  174.1 1.0 copy-start.3
  206.2 6.3 %collective-permute-start = (f32[64,128]{1,0:T(8,128)}, f32[64,128]{1,0:T(8,128)S(1)}, u32[]{:S(2)}, u32[]{:S(2)}) collective-permute-start(f32[64,128]{1,0:T(8,128)} %exit_tile.2), channel_id=1, source_target_pairs={{0,32},{32,64},{64,96},{96,128},{128,160},{160,192},{192,224},{224... | collective-permute-start | bytes 98312 | tf_op jit(solution)/shard_map/ppermute | solution.py:137
  241.5 66.8 %copy-start.9 = (f32[64,128]{1,0:T(8,128)S(1)}, f32[64,128]{1,0:T(8,128)}, u32[]{:S(2)}) copy-start(f32[64,128]{1,0:T(8,128)} %exit_tile.2) | copy-start | bytes 98308
Sparse Core Ops, SparseCore 0:
  152.4 46.4 reduce-scatter.1

commit v2 on v1

--- a/solution.py
+++ b/solution.py
@@ -16,6 +16,22 @@
         left,
         right,
         (((1,), (1,)), ((), ())),
+        precision=lax.Precision.HIGHEST,
+        preferred_element_type=jnp.float32,
+    )
+
+
+def dot_nn(left, right):
+    return jnp.dot(
+        left, right, precision=lax.Precision.HIGHEST, preferred_element_type=jnp.float32
+    )
+
+
+def dot_tn(left, right):
+    return lax.dot_general(
+        left,
+        right,
+        (((0,), (0,)), ((), ())),
         precision=lax.Precision.HIGHEST,
         preferred_element_type=jnp.float32,
     )
@@ -74,50 +90,106 @@
     return jnp.concatenate(out, 0)
 
 
-def exit_kernel(system_ref, right_ref, left_ref, green_ref, out_ref, work):
+def factor_kernel(system_ref, inverse_ref, work):
     count = work.shape[0]
     rows = system_ref.shape[1]
     col_count = system_ref.shape[0] // count
     per = BLOCK // rows
+    size = count * BLOCK
 
     def raw(i, j):
-        return jnp.concatenate(
-            [system_ref[j * col_count + per * i + p] for p in range(per)], 0
-        )
-
-    size = count * BLOCK
+        return jnp.concatenate([system_ref[j * col_count + per * i + p] for p in range(per)], 0)
+
     for j in range(count):
         for i in range(j, count):
             work[j, i * BLOCK : (i + 1) * BLOCK, :] = 0.5 * (raw(i, j) + raw(j, i).T)
-        chunk = jnp.concatenate([right_ref[per * j + p] for p in range(per)], 0)
-        work[j, size : size + BLOCK, :] = chunk.T
-        work[j, size + BLOCK : size + BLOCK + rows, :] = left_ref[j]
     for k in range(count):
         begin = k * BLOCK
-        inverse = inverse_factor(work[k, begin : begin + BLOCK, :])
-        panel = dot_nt(work[k, begin + BLOCK :, :], inverse)
-        for j in range(k + 1, count):
-            lead = (j - k - 1) * BLOCK
-            work[j, j * BLOCK :, :] -= dot_nt(panel[lead:], panel[lead : lead + BLOCK])
-        work[k, size:, :] = panel[size - begin - BLOCK :]
-    total = green_ref[...]
-    for k in range(count):
-        total -= dot_nt(work[k, size + BLOCK :, :], work[k, size : size + BLOCK, :])
-    out_ref[...] = total
-
-
-def exit_tile_of(system, right, left, green):
-    rows = green.shape[0]
-    count = left.shape[0]
+        end = begin + BLOCK
+        inverse = inverse_factor(work[k, begin:end, :])
+        if k + 1 < count:
+            panel = dot_nt(work[k, end:, :], inverse)
+            for j in range(k + 1, count):
+                lead = (j - k - 1) * BLOCK
+                work[j, j * BLOCK :, :] -= dot_nt(panel[lead:], panel[lead : lead + BLOCK])
+            work[k, end:, :] = panel
+        for j in range(k):
+            total = dot_nn(work[j, begin:end, :], inverse_ref[j * BLOCK : (j + 1) * BLOCK, j * BLOCK : (j + 1) * BLOCK])
+            for i in range(j + 1, k):
+                total += dot_nn(
+                    work[i, begin:end, :],
+                    inverse_ref[i * BLOCK : (i + 1) * BLOCK, j * BLOCK : (j + 1) * BLOCK],
+                )
+            inverse_ref[begin:end, j * BLOCK : (j + 1) * BLOCK] = -dot_nn(inverse, total)
+        inverse_ref[begin:end, begin:end] = inverse
+        if k + 1 < count:
+            inverse_ref[begin:end, end:] = jnp.zeros((BLOCK, size - end), jnp.float32)
+
+
+def inverse_factor_of(system, count):
+    rows = system.shape[1]
+    size = count * BLOCK
+    return pl.pallas_call(
+        factor_kernel,
+        out_shape=jax.ShapeDtypeStruct((size, size), jnp.float32),
+        scratch_shapes=[pltpu.VMEM((count, size, BLOCK), jnp.float32)],
+        cost_estimate=pl.CostEstimate(
+            flops=30_000_000_000, bytes_accessed=2_000_000, transcendentals=0
+        ),
+        name="inverse_factor",
+    )(system)
+
+
+def exit_kernel(inverse_ref, right_ref, left_ref, green_ref, out_ref):
+    inverse = inverse_ref[...]
+    right = jnp.concatenate([right_ref[p] for p in range(right_ref.shape[0])], 0)
+    left = jnp.concatenate([left_ref[p] for p in range(left_ref.shape[0])], 1)
+    solved = dot_nn(inverse, right)
+    out_ref[...] = green_ref[...] - dot_nn(dot_nt(left, inverse), solved)
+
+
+def exit_tile_of(inverse, right, left, green):
     return pl.pallas_call(
         exit_kernel,
         out_shape=jax.ShapeDtypeStruct(green.shape, jnp.float32),
-        scratch_shapes=[pltpu.VMEM((count, count * BLOCK + BLOCK + rows, BLOCK), jnp.float32)],
         cost_estimate=pl.CostEstimate(
-            flops=600_000_000, bytes_accessed=2_000_000, transcendentals=0
+            flops=600_000_000, bytes_accessed=1_500_000, transcendentals=0
         ),
         name="exit_tile",
-    )(system, right, left, green)
+    )(inverse, right, left, green)
+
+
+def exit_from_coupling_kernel(place_ref, inverse_ref, coupling_ref, green_ref, out_ref, product):
+    inverse = inverse_ref[...]
+    rows = coupling_ref.shape[1]
+    size = inverse.shape[0]
+    col_count = size // rows
+    per = BLOCK // rows
+    row_index, col_index = place_ref[0], place_ref[1]
+
+    def columns(block):
+        start = block * col_count
+        return jnp.concatenate([coupling_ref[start + p] for p in range(col_count)], 0)
+
+    right = dot_nn(inverse, columns(row_index))
+    left = dot_nn(inverse, columns(col_index // per))
+    product[...] = dot_tn(left, right)
+    half = pl.multiple_of((col_index % per) * rows, rows)
+    out_ref[...] = green_ref[...] - product[pl.ds(half, rows), :]
+
+
+def exit_tile_from_coupling(place, inverse, coupling, green):
+    vmem = pl.BlockSpec(memory_space=pltpu.VMEM)
+    return pl.pallas_call(
+        exit_from_coupling_kernel,
+        out_shape=jax.ShapeDtypeStruct(green.shape, jnp.float32),
+        in_specs=[pl.BlockSpec(memory_space=pltpu.SMEM), vmem, vmem, vmem],
+        scratch_shapes=[pltpu.VMEM((BLOCK, BLOCK), jnp.float32)],
+        cost_estimate=pl.CostEstimate(
+            flops=800_000_000, bytes_accessed=2_500_000, transcendentals=0
+        ),
+        name="exit_tile_from_coupling",
+    )(place, inverse, coupling, green)
 
 
 def contract(left_rows, right_rows):
@@ -148,45 +220,57 @@
     bounds = lax.dynamic_slice_in_dim(radii_table, sec_index, 2)
     sector_width = (bounds[1] - bounds[0]).astype(jnp.float32)
     levels = state_energies[0]
+    place = jnp.stack([lax.axis_index("row"), lax.axis_index("col")]).astype(jnp.int32)
 
     def greens(period):
         energy = plan[0, period].astype(jnp.float32) / ENERGIES
         weight = 8.0 / (sector_width * (levels - energy))
         scaled = (everyone.astype(jnp.float32) * weight).astype(jnp.bfloat16)
-        scaled_own = (own[0].astype(jnp.float32) * weight).astype(jnp.bfloat16)
         paired = own.reshape(2 * tile, own.shape[2])
-        return jnp.concatenate(
-            [
-                contract(scaled[0], paired),
-                contract(scaled[1], own[1]),
-                contract(everyone[1], scaled_own),
-            ],
-            1,
-        )
-
+        blocks = [contract(scaled[0], paired), contract(scaled[1], own[1])]
+        if period == 0:
+            scaled_own = (own[0].astype(jnp.float32) * weight).astype(jnp.bfloat16)
+            blocks.append(contract(everyone[1], scaled_own))
+        full = jnp.concatenate(blocks, 1)
+        return full.reshape(col_count, full.shape[0] // col_count, full.shape[1])
+
+    def by_kind(blocks):
+        return [blocks[:, i : i + tile] for i in range(0, blocks.shape[1], tile)]
+
+    device_count = row_count * col_count
     results = []
+    left_left, left_right, green, crossed = by_kind(
+        lax.all_to_all(greens(0), "col", 0, 0).sum(0)
+    )
+    waiting = [greens(period) for period in range(1, TICKS)]
     boundary = entry_r[0]
-    later = [
-        lax.psum_scatter(greens(period), "col", scatter_dimension=0, tiled=True)
-        for period in range(1, TICKS)
-    ]
-    partial = greens(0)
-    parts = lax.all_to_all(
-        partial.reshape(col_count, -1, partial.shape[1]), "col", 0, 0
-    )
-    blocks = parts.sum(0)
     for period in range(TICKS):
-        right = spread(blocks[:, tile : 2 * tile], "col", col_count)
-        left = spread(blocks[:, 3 * tile :], "row", row_count)
-        system = spread(
-            blocks[:, :tile] + boundary, ("row", "col"), row_count * col_count
-        )
-        exit_tile = exit_tile_of(system, right, left, blocks[:, 2 * tile : 3 * tile])
+        system = spread(left_left + boundary, ("row", "col"), device_count)
+        if period == 0:
+            left = spread(crossed, "row", row_count)
+            system, left, left_right, waiting = lax.optimization_barrier(
+                (system, left, left_right, waiting)
+            )
+            copies = jnp.broadcast_to(left_right[None], (col_count,) + left_right.shape)
+            parts = lax.all_to_all(
+                jnp.concatenate(waiting + [copies], 2), "col", 0, 0
+            )
+            inverse = inverse_factor_of(system, row_count)
+            exit_tile = exit_tile_of(inverse, parts[:, :, -tile:], left, green)
+            summed = parts[:, :, :-tile].sum(0)
+            later = [
+                by_kind(block) for block in jnp.split(summed, TICKS - 1, axis=1)
+            ]
+        else:
+            system, left_right = lax.optimization_barrier((system, left_right))
+            coupling = spread(left_right, ("row", "col"), device_count)
+            inverse = inverse_factor_of(system, row_count)
+            exit_tile = exit_tile_from_coupling(place, inverse, coupling, green)
         results.append(exit_tile)
         if period + 1 < TICKS:
             entering = shifted(exit_tile, "sec", 1)
             boundary = jnp.where(sec_index == 0, fresh_r[period], entering)
-            blocks = later[period]
+            left_left, left_right, green = later[period]
     return jnp.stack(results, 0)[:, None]
 
 

time: 322 us -> 295 us (0.916)
  the two profiles are of different devices: /device:TPU:22 before, /device:TPU:30 now
where the time goes in v2:
time: 295 us; the launch traced here: 290 us
  waiting for transfers between devices  91.4 us (31%)
  Pallas kernels  69.9 us (24%)
  blocking collectives  61.3 us (21%)
  starting transfers between devices  43.9 us (15%)
  local copies, waits for them, and re-layouts  10.9 us (4%)
  other arithmetic  7.08 us (2%)
  between operations  3.02 us (1%)
    all_to_all x4, waiting for transfers between devices, spread(): return lax.all_to_all(copies, axes, 0, 0)  87 us
    pallas_call x2, Pallas kernels, inverse_factor_of(): pl.pallas_call(factor_kernel, out_shape=jax.ShapeDtypeStruct((size, size)...  61.6 us
    all_to_all x4, starting transfers between devices, spread(): return lax.all_to_all(copies, axes, 0, 0)  37.7 us
    all_to_all x1, blocking collectives, local(): lax.all_to_all(greens(0), 'col', 0, 0).sum(0)  33 us
    all_to_all x1, blocking collectives, spread(): return lax.all_to_all(copies, axes, 0, 0)  28.4 us
    broadcast_in_dim x5, local copies, waits for them, and re-layouts, spread(): copies = jnp.broadcast_to(tile[None], (count,) + tile.shape)  6.06 us
  transfers between devices with their start and end apart: 6, of which 5 were waited for; matrix products, arithmetic and copies ran while one was open for 1% of the time, Pallas kernels for 21%

profile of v2, /device:TPU:30, one launch (start us, length us, event | category | flops | bytes accessed | tf_op | source)
XLA Modules:
  0.0 289.9 jit_solution(7784746697406046209)
XLA Ops:
  0.0 2.6 broadcast_in_dim.17
  2.6 15.9 %all-to-all-start = ((bf16[4,2,128,1024]{3,2,1,0:T(8,128)(2,1)}), bf16[4,2,128,1024]{3,2,1,0:T(8,128)(2,1)S(1)}, u32[]{:S(2)}, u32[]{:S(2)}) async-start(bf16[4,2,128,1024]{3,2,1,0:T(8,128)(2,1)} %broadcast_in_dim.17), calls=%async_computation | async-start | bytes 4194304 | tf_op jit(solution)/shard_map/all_to_all | solution.py:203
  22.4 30.3 %all-to-all-done = bf16[4,2,128,1024]{3,2,1,0:T(8,128)(2,1)S(1)} async-done(((bf16[4,2,128,1024]{3,2,1,0:T(8,128)(2,1)}), bf16[4,2,128,1024]{3,2,1,0:T(8,128)(2,1)S(1)}, u32[]{:S(2)}, u32[]{:S(2)}) %all-to-all-start) | async-done | bytes 2097184 | tf_op jit(solution)/shard_map/all_to_all | solution.py:203
  54.5 2.5 fusion.1
  58.4 33.0 %all_to_all.35 = f32[8,64,512]{2,1,0:T(8,128)S(1)} all-to-all(f32[8,64,512]{2,1,0:T(8,128)S(1)} %bitcast.57), channel_id=1, replica_groups=mesh['sec'=32,'row'=4,'col'=8] {'col'}, dimensions={0} | all-to-all | bytes 2097152 | tf_op jit(solution)/shard_map/all_to_all | solution.py:243
  92.1 28.4 %all_to_all.36.left_ref = f32[4,64,128]{2,1,0:T(8,128)} all-to-all(f32[4,64,128]{2,1,0:T(8,128)S(1)} %broadcast_in_dim.19), channel_id=1, replica_groups=mesh['sec'=32,'row'=4,'col'=8] {'row'}, dimensions={0} | all-to-all | bytes 262144 | tf_op jit(solution)/shard_map/all_to_all | solution.py:203
  120.4 1.1 broadcast_in_dim.18
  121.5 5.7 %all-to-all-start.2 = ((f32[32,64,128]{2,1,0:T(8,128)}), f32[32,64,128]{2,1,0:T(8,128)}, u32[]{:S(2)}, u32[]{:S(2)}) async-start(f32[32,64,128]{2,1,0:T(8,128)} %broadcast_in_dim.18), calls=%async_computation.2 | async-start | bytes 2097152 | tf_op jit(solution)/shard_map/all_to_all | solution.py:203
  128.6 25.6 %all-to-all-done.2.system_ref = f32[32,64,128]{2,1,0:T(8,128)} async-done(((f32[32,64,128]{2,1,0:T(8,128)}), f32[32,64,128]{2,1,0:T(8,128)}, u32[]{:S(2)}, u32[]{:S(2)}) %all-to-all-start.2) | async-done | bytes 1048608 | tf_op jit(solution)/shard_map/all_to_all | solution.py:203
  154.2 1.1 pad_maximum_fusion.1
  155.3 4.3 %all-to-all-start.4 = ((f32[8,64,512]{2,1,0:T(8,128)}), f32[8,64,512]{2,1,0:T(8,128)S(1)}, u32[]{:S(2)}, u32[]{:S(2)}) async-start(f32[8,64,512]{2,1,0:T(8,128)} %pad_maximum_fusion.1), calls=%async_computation.4 | async-start | bytes 2097152 | tf_op jit(solution)/shard_map/all_to_all | solution.py:255
  159.5 31.0 %inverse_factor.2.inverse_ref = f32[512,512]{1,0:T(8,128)} custom-call(f32[32,64,128]{2,1,0:T(8,128)} %all-to-all-done.2.system_ref), custom_call_target="tpu_custom_call" | custom-call | flops 30000001024 | bytes 2000000 | tf_op jit(solution)/shard_map/inverse_factor/pallas_call | solution.py:132
  191.2 4.0 %exit_tile.1 = f32[64,128]{1,0:T(8,128)} custom-call(f32[512,512]{1,0:T(8,128)} %inverse_factor.2.inverse_ref, f32[8,64,128]{2,1,0:T(8,128)} %slice.92.right_ref, f32[4,64,128]{2,1,0:T(8,128)} %all_to_all.36.left_ref, f32[64,128]{1,0:T(8,128)} %get-tuple-element.21.green_ref), custom_call_target="tpu_custom_call" | custom-call | flops 600000000 | bytes 1500000 | tf_op jit(solution)/shard_map/exit_tile/pallas_call | solution.py:152
  195.2 1.9 collective-permute-start
  197.2 4.3 %collective-permute-done = f32[64,128]{1,0:T(8,128)S(1)} collective-permute-done((f32[64,128]{1,0:T(8,128)}, f32[64,128]{1,0:T(8,128)S(1)}, u32[]{:S(2)}, u32[]{:S(2)}) %collective-permute-start) | collective-permute-done | bytes 32800 | tf_op jit(solution)/shard_map/ppermute | solution.py:209
  202.2 1.1 broadcast_in_dim.21
  203.3 8.9 %all-to-all-start.5 = ((f32[32,64,128]{2,1,0:T(8,128)}), f32[32,64,128]{2,1,0:T(8,128)S(1)}, u32[]{:S(2)}, u32[]{:S(2)}) async-start(f32[32,64,128]{2,1,0:T(8,128)} %broadcast_in_dim.21), calls=%async_computation.5 | async-start | bytes 2097152 | tf_op jit(solution)/shard_map/all_to_all | solution.py:203
  212.7 30.9 %all-to-all-done.5.system_ref = f32[32,64,128]{2,1,0:T(8,128)S(1)} async-done(((f32[32,64,128]{2,1,0:T(8,128)}), f32[32,64,128]{2,1,0:T(8,128)S(1)}, u32[]{:S(2)}, u32[]{:S(2)}) %all-to-all-start.5) | async-done | bytes 1048608 | tf_op jit(solution)/shard_map/all_to_all | solution.py:203
  243.6 1.2 broadcast_in_dim.22
  244.8 7.2 %all-to-all-start.6 = ((f32[32,64,128]{2,1,0:T(8,128)}), f32[32,64,128]{2,1,0:T(8,128)S(1)}, u32[]{:S(2)}, u32[]{:S(2)}) async-start(f32[32,64,128]{2,1,0:T(8,128)} %broadcast_in_dim.22), calls=%async_computation.6 | async-start | bytes 2097152 | tf_op jit(solution)/shard_map/all_to_all | solution.py:203
  252.1 30.6 %inverse_factor.3.inverse_ref = f32[512,512]{1,0:T(8,128)} custom-call(f32[32,64,128]{2,1,0:T(8,128)} %copy-done.2), custom_call_target="tpu_custom_call" | custom-call | flops 30000001024 | bytes 2000000 | tf_op jit(solution)/shard_map/inverse_factor/pallas_call | solution.py:132
  283.0 1.0 copy-done.3
  284.0 4.3 %exit_tile_from_coupling.1 = f32[64,128]{1,0:T(8,128)} custom-call(s32[2]{0:T(128)} %pad_add_fusion.place_ref, f32[512,512]{1,0:T(8,128)} %inverse_factor.3.inverse_ref, f32[32,64,128]{2,1,0:T(8,128)} %copy-done.3, f32[64,128]{1,0:T(8,128)} %get-tuple-element.25.green_ref), custom_call_target="tpu_custom_call" | custom-call | flops 800000000 | bytes 2500000 | tf_op jit(solution)/shard_map/exit_tile_from_coupling/pallas_call | solution.py:183
  288.3 1.4 maximum_bitcast_fusion
  (44 shorter events, 8.7 us)
Async XLA Ops:
  2.6 15.9 %copy-start.9 = (s32[33]{0:T(128)S(1)}, s32[33]{0:T(128)}, u32[]{:S(2)}) copy-start(s32[33]{0:T(128)} %param.8) | copy-start | bytes 400
  2.6 17.9 %copy-start.8 = (s32[1,2]{1,0:T(1,128)S(1)}, s32[1,2]{1,0:T(1,128)}, u32[]{:S(2)}) copy-start(s32[1,2]{1,0:T(1,128)} %param.9) | copy-start | bytes 28
  2.6 19.8 %copy-start.7 = (f32[1,1024]{1,0:T(1,128)S(1)}, f32[1,1024]{1,0:T(1,128)}, u32[]{:S(2)}) copy-start(f32[1,1024]{1,0:T(1,128)} %param.7) | copy-start | bytes 12292
  2.6 50.1 %all-to-all-start = ((bf16[4,2,128,1024]{3,2,1,0:T(8,128)(2,1)}), bf16[4,2,128,1024]{3,2,1,0:T(8,128)(2,1)S(1)}, u32[]{:S(2)}, u32[]{:S(2)}) async-start(bf16[4,2,128,1024]{3,2,1,0:T(8,128)(2,1)} %broadcast_in_dim.17), calls=%async_computation | async-start | bytes 4194304 | tf_op jit(solution)/shard_map/all_to_all | solution.py:203
  52.9 1.0 copy-start.1
  58.3 33.0 %copy-start.4 = (f32[1,64,128]{2,1,0:T(8,128)S(1)}, f32[1,64,128]{2,1,0:T(8,128)}, u32[]{:S(2)}) copy-start(f32[1,64,128]{2,1,0:T(8,128)} %param.10) | copy-start | bytes 98308
  91.4 35.9 %copy-start = (bf16[2,512,1024]{2,1,0:T(8,128)(2,1)S(1)}, bf16[2,512,1024]{2,1,0:T(8,128)(2,1)}, u32[]{:S(2)}) copy-start(bf16[2,512,1024]{2,1,0:T(8,128)(2,1)} %get-tuple-element.17) | copy-start | bytes 6291460
  121.5 32.6 %all-to-all-start.2 = ((f32[32,64,128]{2,1,0:T(8,128)}), f32[32,64,128]{2,1,0:T(8,128)}, u32[]{:S(2)}, u32[]{:S(2)}) async-start(f32[32,64,128]{2,1,0:T(8,128)} %broadcast_in_dim.18), calls=%async_computation.2 | async-start | bytes 2097152 | tf_op jit(solution)/shard_map/all_to_all | solution.py:203
  155.3 35.2 %all-to-all-start.4 = ((f32[8,64,512]{2,1,0:T(8,128)}), f32[8,64,512]{2,1,0:T(8,128)S(1)}, u32[]{:S(2)}, u32[]{:S(2)}) async-start(f32[8,64,512]{2,1,0:T(8,128)} %pad_maximum_fusion.1), calls=%async_computation.4 | async-start | bytes 2097152 | tf_op jit(solution)/shard_map/all_to_all | solution.py:255
  190.5 11.0 %copy-start.6 = (f32[1,64,128]{2,1,0:T(8,128)S(1)}, f32[1,64,128]{2,1,0:T(8,128)}, u32[]{:S(2)}) copy-start(f32[1,64,128]{2,1,0:T(8,128)} %param.11) | copy-start | bytes 98308
  195.2 6.3 %collective-permute-start = (f32[64,128]{1,0:T(8,128)}, f32[64,128]{1,0:T(8,128)S(1)}, u32[]{:S(2)}, u32[]{:S(2)}) collective-permute-start(f32[64,128]{1,0:T(8,128)} %exit_tile.1), channel_id=1, source_target_pairs={{0,32},{32,64},{64,96},{96,128},{128,160},{160,192},{192,224},{224... | collective-permute-start | bytes 98312 | tf_op jit(solution)/shard_map/ppermute | solution.py:209
  203.3 40.3 %all-to-all-start.5 = ((f32[32,64,128]{2,1,0:T(8,128)}), f32[32,64,128]{2,1,0:T(8,128)S(1)}, u32[]{:S(2)}, u32[]{:S(2)}) async-start(f32[32,64,128]{2,1,0:T(8,128)} %broadcast_in_dim.21), calls=%async_computation.5 | async-start | bytes 2097152 | tf_op jit(solution)/shard_map/all_to_all | solution.py:203
  243.6 8.5 %copy-start.2 = (f32[32,64,128]{2,1,0:T(8,128)}, f32[32,64,128]{2,1,0:T(8,128)S(1)}, u32[]{:S(2)}) copy-start(f32[32,64,128]{2,1,0:T(8,128)S(1)} %all-to-all-done.5.system_ref) | copy-start | bytes 3145732
  244.8 38.2 %all-to-all-start.6 = ((f32[32,64,128]{2,1,0:T(8,128)}), f32[32,64,128]{2,1,0:T(8,128)S(1)}, u32[]{:S(2)}, u32[]{:S(2)}) async-start(f32[32,64,128]{2,1,0:T(8,128)} %broadcast_in_dim.22), calls=%async_computation.6 | async-start | bytes 2097152 | tf_op jit(solution)/shard_map/all_to_all | solution.py:203
  282.7 5.5 %copy-start.5 = (f32[64,128]{1,0:T(8,128)S(1)}, f32[64,128]{1,0:T(8,128)}, u32[]{:S(2)}) copy-start(f32[64,128]{1,0:T(8,128)} %exit_tile.1) | copy-start | bytes 98308
  283.0 1.0 copy-start.3
